TPU v7x, 512 devices: a whole 4x8x8 slice. The times are simulated.
512 devices in a mesh: dp: 32 (over x, y), table: 16 (over z, core).
Axes of the slice: x: 4, y: 8, z: 8, core: 2. Of those that a mesh axis runs over, the one named last changes fastest.
Arguments:
- table: bfloat16 [12288, 512], P('table'), may hold values from -6 to 6
- history_shard: int32 [512, 256, 1], P(('dp', 'table')), may hold values from 0 to 15; in each aligned block of 256 rows (0 to 255, 256 to 511, ..., all dimensions but the last counted through in order) at most 32 rows name the same one
- history_row: int32 [512, 256], P(('dp', 'table')), may hold values from 0 to 767
- lengths: int32 [512], P(('dp', 'table')), may hold values from 1 to 256, 98304 in all
- w_in: bfloat16 [512, 2048], replicated, may hold values from -0.25 to 0.25
- w_out: bfloat16 [512, 512], replicated, may hold values from -0.25 to 0.25
- cotangent: bfloat16 [512, 256, 512], P(('dp', 'table')), may hold values from -6 to 6
Outputs:
- table_grad: float32 [12288, 512], P('table')
- dense_grad: bfloat16 [512, 512], replicated
Inputs may be any that keep to these rules, and one draw needn't show every extreme that they name: `history_shard`: among the 256 history slots of one device's samples, at most 32 name one table shard, and that bound is met by some shard in some device's slots. `lengths`: some sample has the full length 256.
All inputs are finite; a program needn't handle non-finite values. No bound on the sum of `lengths` on one device may be relied on, other than what follows from the above.
Results may differ from a plain program's by a relative error of at most 0.017.
Values may be sent and summed in bfloat16 or wider, within the bound.
A program may use at most 64 MiB of HBM per device.

v0:
```python
import math
import jax
import jax.numpy as jnp
from jax import lax
from jax.sharding import PartitionSpec as P

HEADS = 4


def layer_norm(values):
    average = jnp.mean(values, axis=-1, keepdims=True)
    centred = values - average
    variance = jnp.mean(centred * centred, axis=-1, keepdims=True)
    return centred * lax.rsqrt(variance + 1e-06)


def hstu_layer(embedded, w_in, w_out, lengths):
    samples_here, seq_span, model_width = embedded.shape
    head_dim = model_width // HEADS
    normed = layer_norm(embedded.astype(jnp.float32)).astype(jnp.bfloat16)
    projected = jax.nn.silu(
        jnp.dot(
            normed.reshape(samples_here * seq_span, model_width),
            w_in,
            preferred_element_type=jnp.float32,
        )
    )
    gate_part = projected[:, :model_width]
    shaped = (samples_here, seq_span, HEADS, head_dim)
    values = projected[:, model_width : 2 * model_width].astype(jnp.bfloat16).reshape(shaped)
    queries = projected[:, 2 * model_width : 3 * model_width].astype(jnp.bfloat16).reshape(shaped)
    keys = projected[:, 3 * model_width :].astype(jnp.bfloat16).reshape(shaped)
    scores = jnp.einsum(
        "blhd,bmhd->bhlm", queries.astype(jnp.float32), keys.astype(jnp.float32)
    ) * head_dim ** (-0.5)
    positions = jnp.arange(seq_span)
    live_keys = (positions[None, None, :] <= positions[None, :, None]) & (
        positions[None, None, :] < lengths[:, None, None]
    )
    weights = (
        jnp.where(live_keys[:, None], jax.nn.silu(scores), 0.0)
        / lengths.astype(jnp.float32)[:, None, None, None]
    )
    weights = weights.astype(jnp.bfloat16)
    attended = jnp.einsum(
        "bhlm,bmhd->blhd", weights.astype(jnp.float32), values.astype(jnp.float32)
    ).reshape(samples_here * seq_span, model_width)
    mixed = (layer_norm(attended) * gate_part).astype(jnp.bfloat16)
    output = jnp.dot(mixed, w_out, preferred_element_type=jnp.float32) + embedded.reshape(
        -1, model_width
    ).astype(jnp.float32)
    return (output, mixed)


def pick_rows(index, length):
    return (index[:, None] == jnp.arange(length, dtype=jnp.int32)[None, :]).astype(jnp.bfloat16)


def per_device(table, history_shard, history_row, lengths, w_in, w_out, cotangent):
    shard_rows, model_width = table.shape
    samples_here, seq_span = history_row.shape
    groups = lax.axis_size("table")
    copies = lax.axis_size("dp")
    slot_count = samples_here * seq_span
    capacity = 2 * slot_count // groups
    owners = history_shard[:, :, 0].reshape(-1)
    local_rows = history_row.reshape(-1)
    owner_hits = (owners[:, None] == jnp.arange(groups)[None, :]).astype(jnp.int32)
    slot_rank = jnp.sum((jnp.cumsum(owner_hits, axis=0) - owner_hits) * owner_hits, axis=1)
    position = owners * capacity + slot_rank
    slot_hits = position[:, None] == jnp.arange(groups * capacity, dtype=jnp.int32)[None, :]
    requested = jnp.sum(jnp.where(slot_hits, local_rows[:, None], 0), axis=0).reshape(
        groups, capacity
    )
    incoming = lax.all_to_all(requested, "table", split_axis=0, concat_axis=0, tiled=True).reshape(
        -1
    )
    reply = jnp.dot(
        pick_rows(incoming, shard_rows), table, preferred_element_type=jnp.float32
    ).astype(jnp.bfloat16)
    received = lax.all_to_all(
        reply.reshape(groups, capacity, model_width),
        "table",
        split_axis=0,
        concat_axis=0,
        tiled=True,
    ).reshape(groups * capacity, model_width)
    place = slot_hits.astype(jnp.bfloat16)
    embedded = jnp.dot(place, received, preferred_element_type=jnp.float32).astype(jnp.bfloat16)
    embedded = embedded.reshape(samples_here, seq_span, model_width)
    output, pullback, mixed = jax.vjp(
        lambda rows_in: hstu_layer(rows_in, w_in, w_out, lengths), embedded, has_aux=True
    )
    row_live = jnp.arange(seq_span)[None, :] < lengths[:, None]
    grad_seed = jnp.where(row_live[:, :, None], cotangent, jnp.zeros_like(cotangent))
    flat_seed = grad_seed.reshape(-1, model_width)
    total_slots = slot_count * copies * groups
    grad_scale = 1.0 / math.sqrt(total_slots)
    dense_part = lax.dot_general(
        mixed, flat_seed, (((0,), (0,)), ((), ())), preferred_element_type=jnp.float32
    ).astype(jnp.bfloat16)
    dense_rows = model_width // groups
    dense_terms = lax.all_to_all(
        dense_part.reshape(groups, dense_rows, model_width),
        "table",
        split_axis=0,
        concat_axis=0,
        tiled=True,
    )
    dense_block = jnp.sum(dense_terms.astype(jnp.float32), axis=0).astype(jnp.bfloat16)
    dense_blocks = lax.all_gather(dense_block, "dp", axis=0, tiled=False)
    dense_sum = jnp.sum(dense_blocks.astype(jnp.float32), axis=0) * grad_scale
    dense_grad = lax.all_gather(dense_sum.astype(jnp.bfloat16), "table", axis=0, tiled=True)
    (row_grad,) = pullback(flat_seed.astype(jnp.float32))
    outgoing = lax.dot_general(
        place,
        row_grad.reshape(-1, model_width),
        (((0,), (0,)), ((), ())),
        preferred_element_type=jnp.float32,
    ).astype(jnp.bfloat16)
    arrived = lax.all_to_all(
        outgoing.reshape(groups, capacity, model_width),
        "table",
        split_axis=0,
        concat_axis=0,
        tiled=True,
    ).reshape(groups * capacity, model_width)
    local_grad = lax.dot_general(
        pick_rows(incoming, shard_rows),
        arrived,
        (((0,), (0,)), ((), ())),
        preferred_element_type=jnp.float32,
    ).astype(jnp.bfloat16)
    part_rows = shard_rows // copies
    terms = lax.all_to_all(
        local_grad.reshape(copies, part_rows, model_width),
        "dp",
        split_axis=0,
        concat_axis=0,
        tiled=True,
    )
    summed = jnp.sum(terms.astype(jnp.float32), axis=0).astype(jnp.bfloat16)
    table_grad = lax.all_gather(summed, "dp", axis=0, tiled=True).astype(jnp.float32)
    return (table_grad, dense_grad)


def solution(mesh):
    in_specs = (
        P("table", None),
        P(("dp", "table"), None, None),
        P(("dp", "table"), None),
        P(("dp", "table")),
        P(),
        P(),
        P(("dp", "table"), None, None),
    )
    out_specs = (P("table", None), P())
    return jax.shard_map(
        per_device, mesh=mesh, in_specs=in_specs, out_specs=out_specs, check_vma=False
    )
```

profile of v0, /device:TPU:1, one launch (start us, length us, event | category | flops | bytes accessed | tf_op | source)
XLA Modules:
  0.0 225.5 jit_solution(14855246301839063184)
XLA Ops:
  11.2 18.6 %all_to_all.29 = s32[16,1,32]{2,1,0:T(1,128)S(1)} all-to-all(s32[16,1,32]{2,1,0:T(1,128)S(1)} %all_to_all.18), channel_id=1, replica_groups=mesh['dp'=32,'table'=16] {'table'}, dimensions={0} | all-to-all | bytes 4096 | tf_op jit(solution)/shard_map/all_to_all | solution.py:75
  31.1 2.5 %fusion.17 = bf16[512,512]{1,0:T(8,128)(2,1)} fusion(bf16[768,512]{1,0:T(8,128)(2,1)} %param.7, s32[512]{0:T(512)S(1)} %eq.68), kind=kOutput, calls=%fused_computation.23 | convolution fusion | flops 403308544 | bytes 1312768 | tf_op jit(solution)/shard_map/dot_general | solution.py:78
  33.6 4.0 %all-to-all-start.1 = ((bf16[16,32,512]{2,1,0:T(8,128)(2,1)}), bf16[16,32,512]{2,1,0:T(8,128)(2,1)S(1)}, u32[]{:S(2)}, u32[]{:S(2)}) async-start(bf16[16,32,512]{2,1,0:T(8,128)(2,1)} %bitcast.6), calls=%async_computation.1 | async-start | bytes 1048576 | tf_op jit(solution)/shard_map/all_to_all | solution.py:81
  38.4 16.6 %all-to-all-done.1 = bf16[16,32,512]{2,1,0:T(8,128)(2,1)S(1)} async-done(((bf16[16,32,512]{2,1,0:T(8,128)(2,1)}), bf16[16,32,512]{2,1,0:T(8,128)(2,1)S(1)}, u32[]{:S(2)}, u32[]{:S(2)}) %all-to-all-start.1) | async-done | bytes 524320 | tf_op jit(solution)/shard_map/all_to_all | solution.py:81
  55.7 2.7 %fusion.70 = (bf16[256,2048]{1,0:T(8,128)(2,1)S(1)}, f32[256,2048]{1,0:T(8,128)}, f32[256,2048]{1,0:T(8,128)}) fusion(bf16[512,2048]{1,0:T(8,128)(2,1)S(1)} %copy-done, f32[256,512]{1,0:T(8,128)S(1)} %get-tuple-element.15, f32[256]{0:T(256)S(1)} %fusion.63, f32[256]{0:T(256)S(1)} %broadcast_multiply_fusion.1), kind=kOutput, calls=%fused_computation.113 | convolution fusion | flops 539885568 | bytes 7866368 | tf_op jit(solution)/shard_map/jvp()/dot_general | solution.py:22
  60.0 1.6 divide_convert_fusion
  62.7 1.2 copy.48
  64.0 1.8 multiply_reduce_fusion.1
  65.9 1.3 convolution_convert_fusion.1
  68.4 1.3 fusion.76
  69.7 2.0 fusion.31
  73.9 1.9 copy.50
  76.6 4.1 %all-to-all-start.4 = ((bf16[16,32,512]{2,1,0:T(8,128)(2,1)}), bf16[16,32,512]{2,1,0:T(8,128)(2,1)}, u32[]{:S(2)}, u32[]{:S(2)}) async-start(bf16[16,32,512]{2,1,0:T(8,128)(2,1)} %bitcast.30), calls=%async_computation.4 | async-start | bytes 1048576 | tf_op jit(solution)/shard_map/all_to_all | solution.py:103
  80.7 2.9 %multiply_reduce_fusion = (f32[256]{0:T(256)S(1)}, f32[256,512]{1,0:T(8,128)S(1)}) fusion(f32[256,512]{1,0:T(8,128)S(1)} %get-tuple-element.15, f32[256]{0:T(256)S(1)} %broadcast_multiply_fusion.1, bf16[512,2048]{1,0:T(8,128)(2,1)S(1)} %copy-done, f32[256,2048]{1,0:T(8,128)} %get-tuple-element.16, f32[256,512]{1,0:T(8,128)} %get-tuple-element.8, ...), kind=kOutput, calls=%fused_computation.56 | convolution fusion | flops 545390336 | bytes 6555648 | tf_op jit(solution)/shard_map/transpose(jvp())/dot_general | solution.py:22
  84.0 1.3 convolution_convert_fusion.2
  85.3 11.7 %all-to-all-done.4 = bf16[16,32,512]{2,1,0:T(8,128)(2,1)} async-done(((bf16[16,32,512]{2,1,0:T(8,128)(2,1)}), bf16[16,32,512]{2,1,0:T(8,128)(2,1)}, u32[]{:S(2)}, u32[]{:S(2)}) %all-to-all-start.4) | async-done | bytes 524320 | tf_op jit(solution)/shard_map/all_to_all | solution.py:103
  96.9 3.5 %all-to-all-start.2 = ((bf16[16,32,512]{2,1,0:T(8,128)(2,1)}), bf16[16,32,512]{2,1,0:T(8,128)(2,1)S(1)}, u32[]{:S(2)}, u32[]{:S(2)}) async-start(bf16[16,32,512]{2,1,0:T(8,128)(2,1)} %bitcast.27), calls=%async_computation.2 | async-start | bytes 1048576 | tf_op jit(solution)/shard_map/all_to_all | solution.py:121
  100.5 1.7 reduce_sum.150
  102.2 14.9 %all-to-all-done.2 = bf16[16,32,512]{2,1,0:T(8,128)(2,1)S(1)} async-done(((bf16[16,32,512]{2,1,0:T(8,128)(2,1)}), bf16[16,32,512]{2,1,0:T(8,128)(2,1)S(1)}, u32[]{:S(2)}, u32[]{:S(2)}) %all-to-all-start.2) | async-done | bytes 524320 | tf_op jit(solution)/shard_map/all_to_all | solution.py:121
  117.8 31.6 %all_to_all.30 = bf16[32,24,512]{2,1,0:T(8,128)(2,1)S(1)} all-to-all(bf16[32,24,512]{2,1,0:T(8,128)(2,1)S(1)} %bitcast.113), channel_id=1, replica_groups=mesh['dp'=32,'table'=16] {'dp'}, dimensions={0} | all-to-all | bytes 1572864 | tf_op jit(solution)/shard_map/all_to_all | solution.py:135
  149.5 40.4 %all_gather.12 = bf16[768,512]{1,0:T(8,128)(2,1)S(1)} all-gather(bf16[24,512]{1,0:T(8,128)(2,1)S(1)} %reduce_sum.149), channel_id=1, replica_groups=mesh['dp'=32,'table'=16] {'dp'}, dimensions={0}, use_global_device_ids=true | all-gather | bytes 811008 | tf_op jit(solution)/shard_map/all_gather | solution.py:143
  189.9 1.4 convert_element_type.164
  191.3 1.4 convert_reduce_fusion
  192.7 25.2 %all_gather.15 = bf16[512,512]{1,0:T(8,128)(2,1)S(1)} all-gather(bf16[32,512]{1,0:T(8,128)(2,1)S(1)} %multiply_convert_fusion.4), channel_id=1, replica_groups=mesh['dp'=32,'table'=16] {'table'}, dimensions={0}, use_global_device_ids=true | all-gather | bytes 557056 | tf_op jit(solution)/shard_map/all_gather | solution.py:113
  (65 shorter events, 15.0 us)
Async XLA Ops:
  7.2 48.5 %copy-start = (bf16[512,2048]{1,0:T(8,128)(2,1)S(1)}, bf16[512,2048]{1,0:T(8,128)(2,1)}, u32[]{:S(2)}) copy-start(bf16[512,2048]{1,0:T(8,128)(2,1)} %param.11) | copy-start | bytes 6291460
  33.6 21.4 %all-to-all-start.1 = ((bf16[16,32,512]{2,1,0:T(8,128)(2,1)}), bf16[16,32,512]{2,1,0:T(8,128)(2,1)S(1)}, u32[]{:S(2)}, u32[]{:S(2)}) async-start(bf16[16,32,512]{2,1,0:T(8,128)(2,1)} %bitcast.6), calls=%async_computation.1 | async-start | bytes 1048576 | tf_op jit(solution)/shard_map/all_to_all | solution.py:81
  59.3 0.7 copy-start.5
  59.4 2.1 copy-start.7
  60.0 1.6 copy-start.9
  61.6 0.8 copy-start.3
  61.6 2.4 %copy-start.2 = (bf16[1,256,512]{2,1,0:T(8,128)(2,1)S(1)}, bf16[1,256,512]{2,1,0:T(8,128)(2,1)}, u32[]{:S(2)}) copy-start(bf16[1,256,512]{2,1,0:T(8,128)(2,1)} %param.13) | copy-start | bytes 786436
  61.9 0.8 copy-start.1
  64.0 1.9 copy-start.4
  69.7 2.1 copy-start.6
  69.7 2.4 %copy-start.8 = (bf16[256,512]{0,1:T(8,128)(2,1)S(1)}, bf16[256,512]{0,1:T(8,128)(2,1)}, u32[]{:S(2)}) copy-start(bf16[256,512]{0,1:T(8,128)(2,1)} %copy-done.7) | copy-start | bytes 786436
  73.9 6.9 %copy-start.10 = (bf16[256,512]{1,0:T(8,128)(2,1)S(1)}, bf16[256,512]{1,0:T(8,128)(2,1)}, u32[]{:S(2)}) copy-start(bf16[256,512]{1,0:T(8,128)(2,1)} %copy.52) | copy-start | bytes 786436
  76.6 20.3 %all-to-all-start.4 = ((bf16[16,32,512]{2,1,0:T(8,128)(2,1)}), bf16[16,32,512]{2,1,0:T(8,128)(2,1)}, u32[]{:S(2)}, u32[]{:S(2)}) async-start(bf16[16,32,512]{2,1,0:T(8,128)(2,1)} %bitcast.30), calls=%async_computation.4 | async-start | bytes 1048576 | tf_op jit(solution)/shard_map/all_to_all | solution.py:103
  96.9 20.2 %all-to-all-start.2 = ((bf16[16,32,512]{2,1,0:T(8,128)(2,1)}), bf16[16,32,512]{2,1,0:T(8,128)(2,1)S(1)}, u32[]{:S(2)}, u32[]{:S(2)}) async-start(bf16[16,32,512]{2,1,0:T(8,128)(2,1)} %bitcast.27), calls=%async_computation.2 | async-start | bytes 1048576 | tf_op jit(solution)/shard_map/all_to_all | solution.py:121
  100.4 90.9 %all-gather.3.cloned.1.call-start = ((), (), s32[]{:S(2)}) async-start(), calls=%async_computation.5 | async-start | bytes 1081344 | tf_op jit(solution)/shard_map/all_gather | solution.py:111
Sparse Core Ops, SparseCore 0:
  104.4 79.3 all-gather.2
where the time goes:
time: 226 us
  blocking collectives  116 us (51%)
  waiting for transfers between devices  43.2 us (19%)
  matrix products  20.1 us (9%)
  between operations  14.9 us (7%)
  starting transfers between devices  11.7 us (5%)
  other arithmetic  10.8 us (5%)
  local copies, waits for them, and re-layouts  8.98 us (4%)
    all_gather x1, blocking collectives, per_device(): lax.all_gather(summed, 'dp', axis=0, tiled=True).astype(jnp.float32)  40.4 us
    all_to_all x1, blocking collectives, per_device(): lax.all_to_all(local_grad.reshape(copies, part_rows, model_width), 'dp',...  31.6 us
    all_gather x1, blocking collectives, per_device(): lax.all_gather(dense_sum.astype(jnp.bfloat16), 'table', axis=0, tiled=True)  25.2 us
    all_to_all x1, blocking collectives, per_device(): lax.all_to_all(requested, 'table', split_axis=0, concat_axis=0, tiled=True)  18.6 us
    all_to_all x1, waiting for transfers between devices, per_device(): lax.all_to_all(reply.reshape(groups, capacity, model_width), 'table', spl...  16.6 us
    all_to_all x1, waiting for transfers between devices, per_device(): lax.all_to_all(outgoing.reshape(groups, capacity, model_width), 'table',...  14.9 us
    all_to_all x1, waiting for transfers between devices, per_device(): lax.all_to_all(dense_part.reshape(groups, dense_rows, model_width), 'tabl...  11.7 us
    dot_general x2, matrix products, hstu_layer(): jnp.dot(normed.reshape(samples_here * seq_span, model_width), w_in, prefe...  5.66 us
  transfers between devices with their start and end apart: 4, of which 3 were waited for; matrix products, arithmetic and copies ran while one was open for 4% of the time, Pallas kernels for 0%

commit v1 on v0

--- a/solution.py
+++ b/solution.py
@@ -57,6 +57,31 @@
 
 
 def per_device(table, history_shard, history_row, lengths, w_in, w_out, cotangent):
+
+    def review_loops(incoming_x, across):
+        u1 = lax.axis_size(across)
+        taken_in = lax.axis_index(across)
+        all_values, x_next, oldest = (u1, taken_in, incoming_x.shape[0])
+        chunks = [q * all_values if i == 0 else q for i, q in enumerate(incoming_x.shape)]
+        block_last = jnp.zeros(chunks, incoming_x.dtype)
+        piece_out = lax.dynamic_update_slice_in_dim(block_last, incoming_x, x_next * oldest, axis=0)
+        back = later = incoming_x
+        for k in range(1, all_values // 2 + 1):
+            back = lax.ppermute(
+                back, across, [(i, (i + 1) % all_values) for i in range(all_values)]
+            )
+            piece_out = lax.dynamic_update_slice_in_dim(
+                piece_out, back, (x_next - k) % all_values * oldest, axis=0
+            )
+            if 2 * k < all_values:
+                later = lax.ppermute(
+                    later, across, [(i, (i - 1) % all_values) for i in range(all_values)]
+                )
+                piece_out = lax.dynamic_update_slice_in_dim(
+                    piece_out, later, (x_next + k) % all_values * oldest, axis=0
+                )
+        return piece_out
+
     shard_rows, model_width = table.shape
     samples_here, seq_span = history_row.shape
     groups = lax.axis_size("table")
@@ -110,7 +135,7 @@
     dense_block = jnp.sum(dense_terms.astype(jnp.float32), axis=0).astype(jnp.bfloat16)
     dense_blocks = lax.all_gather(dense_block, "dp", axis=0, tiled=False)
     dense_sum = jnp.sum(dense_blocks.astype(jnp.float32), axis=0) * grad_scale
-    dense_grad = lax.all_gather(dense_sum.astype(jnp.bfloat16), "table", axis=0, tiled=True)
+    dense_grad = review_loops(dense_sum.astype(jnp.bfloat16), "table")
     (row_grad,) = pullback(flat_seed.astype(jnp.float32))
     outgoing = lax.dot_general(
         place,

time: 226 us -> 291 us (1.29)
  waiting for transfers between devices: 43.2 us -> 111 us
  blocking collectives: 116 us -> 55.2 us
  starting transfers between devices: 11.7 us -> 58.1 us
  matrix products: 20.1 us -> 24.3 us
    ppermute x0 -> x15, starting transfers between devices: none -> 37.4 us  [the longest x8 24.1 us: review_loops(): lax.ppermute(back, across, [(i, (i + 1) % all_values) for i in range(all_...]
    all_gather x1, waiting for transfers between devices: 0.01 us -> 33.3 us  [per_device(): dense_blocks = lax.all_gather(dense_block, 'dp', axis=0, tiled=False)]
    all_to_all x1 -> x0, blocking collectives: 31.6 us -> none  [per_device(): lax.all_to_all(local_grad.reshape(copies, part_rows, model_width), 'dp',...]
    all_gather x1 -> x0, blocking collectives: 25.2 us -> none  [per_device(): lax.all_gather(dense_sum.astype(jnp.bfloat16), 'table', axis=0, tiled=True)]
    all_to_all x0 -> x1, waiting for transfers between devices: none -> 22.8 us  [per_device(): lax.all_to_all(local_grad.reshape(copies, part_rows, model_width), 'dp',...]
    ppermute x0 -> x15, waiting for transfers between devices: none -> 10.2 us  [the longest x8 8.77 us: review_loops(): lax.ppermute(back, across, [(i, (i + 1) % all_values) for i in range(all_...]
    all_to_all x0 -> x1, starting transfers between devices: none -> 9.67 us  [per_device(): lax.all_to_all(local_grad.reshape(copies, part_rows, model_width), 'dp',...]
    all_gather x1, blocking collectives: 40.4 us -> 36.6 us  [per_device(): lax.all_gather(summed, 'dp', axis=0, tiled=True).astype(jnp.float32)]
  transfers between devices with their start and end apart: 4 -> 20, of which waited for: 3 -> 18; matrix products, arithmetic and copies ran while one was open for 4% -> 3% of each run, Pallas kernels for 0% -> 0%
where the time goes in v1:
time: 291 us; the launch traced here: 288 us
  waiting for transfers between devices  111 us (38%)
  starting transfers between devices  58.1 us (20%)
  blocking collectives  55.2 us (19%)
  matrix products  24.3 us (8%)
  between operations  15.2 us (5%)
  other arithmetic  12.6 us (4%)
  local copies, waits for them, and re-layouts  11.8 us (4%)
    all_gather x1, blocking collectives, per_device(): lax.all_gather(summed, 'dp', axis=0, tiled=True).astype(jnp.float32)  36.6 us
    all_gather x1, waiting for transfers between devices, per_device(): dense_blocks = lax.all_gather(dense_block, 'dp', axis=0, tiled=False)  33.3 us
    ppermute x8, starting transfers between devices, review_loops(): lax.ppermute(back, across, [(i, (i + 1) % all_values) for i in range(all_...  24.1 us
    all_to_all x1, waiting for transfers between devices, per_device(): lax.all_to_all(local_grad.reshape(copies, part_rows, model_width), 'dp',...  22.8 us
    all_to_all x1, blocking collectives, per_device(): lax.all_to_all(requested, 'table', split_axis=0, concat_axis=0, tiled=True)  18.6 us
    all_to_all x1, waiting for transfers between devices, per_device(): lax.all_to_all(reply.reshape(groups, capacity, model_width), 'table', spl...  16.6 us
    all_to_all x1, waiting for transfers between devices, per_device(): lax.all_to_all(outgoing.reshape(groups, capacity, model_width), 'table',...  16 us
    ppermute x7, starting transfers between devices, review_loops(): lax.ppermute(later, across, [(i, (i - 1) % all_values) for i in range(all...  13.3 us
  transfers between devices with their start and end apart: 20, of which 18 were waited for; matrix products, arithmetic and copies ran while one was open for 3% of the time, Pallas kernels for 0%

profile of v1, /device:TPU:1, one launch (start us, length us, event | category | flops | bytes accessed | tf_op | source)
XLA Modules:
  0.0 288.3 jit_solution(2841930398637283813)
XLA Ops:
  11.2 18.6 %all_to_all.29 = s32[16,1,32]{2,1,0:T(1,128)S(1)} all-to-all(s32[16,1,32]{2,1,0:T(1,128)S(1)} %all_to_all.18), channel_id=1, replica_groups=mesh['dp'=32,'table'=16] {'table'}, dimensions={0} | all-to-all | bytes 4096 | tf_op jit(solution)/shard_map/all_to_all | solution.py:100
  31.1 2.5 fusion.17
  33.6 4.0 %all-to-all-start.1 = ((bf16[16,32,512]{2,1,0:T(8,128)(2,1)}), bf16[16,32,512]{2,1,0:T(8,128)(2,1)S(1)}, u32[]{:S(2)}, u32[]{:S(2)}) async-start(bf16[16,32,512]{2,1,0:T(8,128)(2,1)} %bitcast.6), calls=%async_computation.1 | async-start | bytes 1048576 | tf_op jit(solution)/shard_map/all_to_all | solution.py:106
  38.4 16.6 %all-to-all-done.1 = bf16[16,32,512]{2,1,0:T(8,128)(2,1)S(1)} async-done(((bf16[16,32,512]{2,1,0:T(8,128)(2,1)}), bf16[16,32,512]{2,1,0:T(8,128)(2,1)S(1)}, u32[]{:S(2)}, u32[]{:S(2)}) %all-to-all-start.1) | async-done | bytes 524320 | tf_op jit(solution)/shard_map/all_to_all | solution.py:106
  55.7 2.7 fusion.70
  71.4 2.1 fusion.76
  73.5 2.1 fusion.31
  77.6 2.3 convolution_convert_fusion.1
  85.3 3.5 %all-to-all-start.4 = ((bf16[16,32,512]{2,1,0:T(8,128)(2,1)}), bf16[16,32,512]{2,1,0:T(8,128)(2,1)S(1)}, u32[]{:S(2)}, u32[]{:S(2)}) async-start(bf16[16,32,512]{2,1,0:T(8,128)(2,1)} %bitcast.102), calls=%async_computation.4 | async-start | bytes 1048576 | tf_op jit(solution)/shard_map/all_to_all | solution.py:128
  88.8 3.0 %multiply_reduce_fusion = (f32[256]{0:T(256)S(1)}, f32[256,512]{1,0:T(8,128)S(1)}) fusion(f32[256,512]{1,0:T(8,128)S(1)} %get-tuple-element.17, f32[256]{0:T(256)S(1)} %broadcast_multiply_fusion.1, bf16[512,2048]{1,0:T(8,128)(2,1)S(1)} %copy-done, f32[256,2048]{1,0:T(8,128)} %get-tuple-element.18, f32[256,512]{1,0:T(8,128)} %get-tuple-element.10, ...), kind=kOutput, calls=%fused_computation.56 | convolution fusion | flops 545390336 | bytes 6555648 | tf_op jit(solution)/shard_map/transpose(jvp())/dot_general | solution.py:22
  93.4 12.1 %all-to-all-done.4 = bf16[16,32,512]{2,1,0:T(8,128)(2,1)S(1)} async-done(((bf16[16,32,512]{2,1,0:T(8,128)(2,1)}), bf16[16,32,512]{2,1,0:T(8,128)(2,1)S(1)}, u32[]{:S(2)}, u32[]{:S(2)}) %all-to-all-start.4) | async-done | bytes 524320 | tf_op jit(solution)/shard_map/all_to_all | solution.py:128
  105.5 3.5 %all-to-all-start.2 = ((bf16[16,32,512]{2,1,0:T(8,128)(2,1)}), bf16[16,32,512]{2,1,0:T(8,128)(2,1)S(1)}, u32[]{:S(2)}, u32[]{:S(2)}) async-start(bf16[16,32,512]{2,1,0:T(8,128)(2,1)} %bitcast.27), calls=%async_computation.2 | async-start | bytes 1048576 | tf_op jit(solution)/shard_map/all_to_all | solution.py:146
  109.7 16.0 %all-to-all-done.2 = bf16[16,32,512]{2,1,0:T(8,128)(2,1)S(1)} async-done(((bf16[16,32,512]{2,1,0:T(8,128)(2,1)}), bf16[16,32,512]{2,1,0:T(8,128)(2,1)S(1)}, u32[]{:S(2)}, u32[]{:S(2)}) %all-to-all-start.2) | async-done | bytes 524320 | tf_op jit(solution)/shard_map/all_to_all | solution.py:146
  127.3 9.7 %all-to-all-start.3 = ((bf16[32,24,512]{2,1,0:T(8,128)(2,1)}), bf16[32,24,512]{2,1,0:T(8,128)(2,1)S(1)}, u32[]{:S(2)}, u32[]{:S(2)}) async-start(bf16[32,24,512]{2,1,0:T(8,128)(2,1)} %bitcast.114), calls=%async_computation.3 | async-start | bytes 1572864 | tf_op jit(solution)/shard_map/all_to_all | solution.py:160
  137.3 22.8 %all-to-all-done.3 = bf16[32,24,512]{2,1,0:T(8,128)(2,1)S(1)} async-done(((bf16[32,24,512]{2,1,0:T(8,128)(2,1)}), bf16[32,24,512]{2,1,0:T(8,128)(2,1)S(1)}, u32[]{:S(2)}, u32[]{:S(2)}) %all-to-all-start.3) | async-done | bytes 786464 | tf_op jit(solution)/shard_map/all_to_all | solution.py:160
  160.2 33.3 %all-gather.3.cloned.1.call-done = bf16[1024,512]{1,0:T(8,128)(2,1)} async-done(((bf16[32,512]{1,0:T(8,128)(2,1)}), bf16[1024,512]{1,0:T(8,128)(2,1)}) %all-gather.3.cloned.1.call-update) | async-done | bytes 1048592 | tf_op jit(solution)/shard_map/all_gather | solution.py:136
  195.0 6.3 %collective-permute-start = (bf16[32,512]{1,0:T(8,128)(2,1)S(1)}, bf16[32,512]{1,0:T(8,128)(2,1)S(1)}, u32[]{:S(2)}, u32[]{:S(2)}) collective-permute-start(bf16[32,512]{1,0:T(8,128)(2,1)S(1)} %get-tuple-element.3), channel_id=1, source_target_pairs={{0,1},{1,2},{2,3},{3,4},{4,5},{5,6},{6,7},{7,8},{8,9},{9,10},{10,1... | collective-permute-start | bytes 98312 | tf_op jit(solution)/shard_map/ppermute | solution.py:70
  201.3 36.6 %all_gather.9 = bf16[768,512]{1,0:T(8,128)(2,1)S(1)} all-gather(bf16[24,512]{1,0:T(8,128)(2,1)S(1)} %reduce_sum.149), channel_id=1, replica_groups=mesh['dp'=32,'table'=16] {'dp'}, dimensions={0}, use_global_device_ids=true | all-gather | bytes 811008 | tf_op jit(solution)/shard_map/all_gather | solution.py:168
  239.2 13.6 %collective-permute-start.2 = (bf16[32,512]{1,0:T(8,128)(2,1)S(1)}, bf16[32,512]{1,0:T(8,128)(2,1)S(1)}, u32[]{:S(2)}, u32[]{:S(2)}) collective-permute-start(bf16[32,512]{1,0:T(8,128)(2,1)S(1)} %collective-permute-done), channel_id=1, source_target_pairs={{0,1},{1,2},{2,3},{3,4},{4,5},{5,6},{6,7},{7,8},{8,9},{9,10},{10,1... | collective-permute-start | bytes 98312 | tf_op jit(solution)/shard_map/ppermute | solution.py:70
  253.8 2.3 collective-permute-start.4
  263.1 3.2 %collective-permute-start.9 = (bf16[32,512]{1,0:T(8,128)(2,1)S(1)}, bf16[32,512]{1,0:T(8,128)(2,1)S(1)}, u32[]{:S(2)}, u32[]{:S(2)}) collective-permute-start(bf16[32,512]{1,0:T(8,128)(2,1)S(1)} %collective-permute-done.7), channel_id=1, source_target_pairs={{0,15},{1,0},{2,1},{3,2},{4,3},{5,4},{6,5},{7,6},{8,7},{9,8},{10,9... | collective-permute-start | bytes 98312 | tf_op jit(solution)/shard_map/ppermute | solution.py:77
  267.2 3.7 %collective-permute-start.11 = (bf16[32,512]{1,0:T(8,128)(2,1)S(1)}, bf16[32,512]{1,0:T(8,128)(2,1)S(1)}, u32[]{:S(2)}, u32[]{:S(2)}) collective-permute-start(bf16[32,512]{1,0:T(8,128)(2,1)S(1)} %collective-permute-done.9), channel_id=1, source_target_pairs={{0,15},{1,0},{2,1},{3,2},{4,3},{5,4},{6,5},{7,6},{8,7},{9,8},{10,9... | collective-permute-start | bytes 98312 | tf_op jit(solution)/shard_map/ppermute | solution.py:77
  271.7 3.7 %collective-permute-start.13 = (bf16[32,512]{1,0:T(8,128)(2,1)S(1)}, bf16[32,512]{1,0:T(8,128)(2,1)S(1)}, u32[]{:S(2)}, u32[]{:S(2)}) collective-permute-start(bf16[32,512]{1,0:T(8,128)(2,1)S(1)} %collective-permute-done.11), channel_id=1, source_target_pairs={{0,15},{1,0},{2,1},{3,2},{4,3},{5,4},{6,5},{7,6},{8,7},{9,8},{10,9... | collective-permute-start | bytes 98312 | tf_op jit(solution)/shard_map/ppermute | solution.py:77
  276.3 4.4 %collective-permute-done.14 = bf16[32,512]{1,0:T(8,128)(2,1)S(1)} collective-permute-done((bf16[32,512]{1,0:T(8,128)(2,1)S(1)}, bf16[32,512]{1,0:T(8,128)(2,1)S(1)}, u32[]{:S(2)}, u32[]{:S(2)}) %collective-permute-start.14) | collective-permute-done | bytes 32800 | tf_op jit(solution)/shard_map/ppermute | solution.py:70
  (106 shorter events, 44.4 us)
Async XLA Ops:
  7.2 48.5 %copy-start = (bf16[512,2048]{1,0:T(8,128)(2,1)S(1)}, bf16[512,2048]{1,0:T(8,128)(2,1)}, u32[]{:S(2)}) copy-start(bf16[512,2048]{1,0:T(8,128)(2,1)} %param.11) | copy-start | bytes 6291460
  33.6 21.4 %all-to-all-start.1 = ((bf16[16,32,512]{2,1,0:T(8,128)(2,1)}), bf16[16,32,512]{2,1,0:T(8,128)(2,1)S(1)}, u32[]{:S(2)}, u32[]{:S(2)}) async-start(bf16[16,32,512]{2,1,0:T(8,128)(2,1)} %bitcast.6), calls=%async_computation.1 | async-start | bytes 1048576 | tf_op jit(solution)/shard_map/all_to_all | solution.py:106
  59.4 2.1 copy-start.5
  61.6 3.5 %copy-start.1 = (bf16[1,256,512]{2,1,0:T(8,128)(2,1)S(1)}, bf16[1,256,512]{2,1,0:T(8,128)(2,1)}, u32[]{:S(2)}) copy-start(bf16[1,256,512]{2,1,0:T(8,128)(2,1)} %param.13) | copy-start | bytes 786436
  73.5 3.1 %copy-start.4 = (bf16[256,512]{0,1:T(8,128)(2,1)S(1)}, bf16[256,512]{0,1:T(8,128)(2,1)}, u32[]{:S(2)}) copy-start(bf16[256,512]{0,1:T(8,128)(2,1)} %copy-done.3) | copy-start | bytes 786436
  85.3 20.2 %all-to-all-start.4 = ((bf16[16,32,512]{2,1,0:T(8,128)(2,1)}), bf16[16,32,512]{2,1,0:T(8,128)(2,1)S(1)}, u32[]{:S(2)}, u32[]{:S(2)}) async-start(bf16[16,32,512]{2,1,0:T(8,128)(2,1)} %bitcast.102), calls=%async_computation.4 | async-start | bytes 1048576 | tf_op jit(solution)/shard_map/all_to_all | solution.py:128
  105.5 20.2 %all-to-all-start.2 = ((bf16[16,32,512]{2,1,0:T(8,128)(2,1)}), bf16[16,32,512]{2,1,0:T(8,128)(2,1)S(1)}, u32[]{:S(2)}, u32[]{:S(2)}) async-start(bf16[16,32,512]{2,1,0:T(8,128)(2,1)} %bitcast.27), calls=%async_computation.2 | async-start | bytes 1048576 | tf_op jit(solution)/shard_map/all_to_all | solution.py:146
  109.0 84.6 %all-gather.3.cloned.1.call-start = ((), (), s32[]{:S(2)}) async-start(), calls=%async_computation.5 | async-start | bytes 1081344 | tf_op jit(solution)/shard_map/all_gather | solution.py:136
  127.3 32.8 %all-to-all-start.3 = ((bf16[32,24,512]{2,1,0:T(8,128)(2,1)}), bf16[32,24,512]{2,1,0:T(8,128)(2,1)S(1)}, u32[]{:S(2)}, u32[]{:S(2)}) async-start(bf16[32,24,512]{2,1,0:T(8,128)(2,1)} %bitcast.114), calls=%async_computation.3 | async-start | bytes 1572864 | tf_op jit(solution)/shard_map/all_to_all | solution.py:160
  195.0 44.2 %collective-permute-start = (bf16[32,512]{1,0:T(8,128)(2,1)S(1)}, bf16[32,512]{1,0:T(8,128)(2,1)S(1)}, u32[]{:S(2)}, u32[]{:S(2)}) collective-permute-start(bf16[32,512]{1,0:T(8,128)(2,1)S(1)} %get-tuple-element.3), channel_id=1, source_target_pairs={{0,1},{1,2},{2,3},{3,4},{4,5},{5,6},{6,7},{7,8},{8,9},{9,10},{10,1... | collective-permute-start | bytes 98312 | tf_op jit(solution)/shard_map/ppermute | solution.py:70
  201.3 51.5 %collective-permute-start.1 = (bf16[32,512]{1,0:T(8,128)(2,1)S(1)}, bf16[32,512]{1,0:T(8,128)(2,1)S(1)}, u32[]{:S(2)}, u32[]{:S(2)}) collective-permute-start(bf16[32,512]{1,0:T(8,128)(2,1)S(1)} %get-tuple-element.3), channel_id=1, source_target_pairs={{0,15},{1,0},{2,1},{3,2},{4,3},{5,4},{6,5},{7,6},{8,7},{9,8},{10,9... | collective-permute-start | bytes 98312 | tf_op jit(solution)/shard_map/ppermute | solution.py:77
  239.2 14.6 %collective-permute-start.2 = (bf16[32,512]{1,0:T(8,128)(2,1)S(1)}, bf16[32,512]{1,0:T(8,128)(2,1)S(1)}, u32[]{:S(2)}, u32[]{:S(2)}) collective-permute-start(bf16[32,512]{1,0:T(8,128)(2,1)S(1)} %collective-permute-done), channel_id=1, source_target_pairs={{0,1},{1,2},{2,3},{3,4},{4,5},{5,6},{6,7},{7,8},{8,9},{9,10},{10,1... | collective-permute-start | bytes 98312 | tf_op jit(solution)/shard_map/ppermute | solution.py:70
  252.8 3.6 %collective-permute-start.3 = (bf16[32,512]{1,0:T(8,128)(2,1)S(1)}, bf16[32,512]{1,0:T(8,128)(2,1)S(1)}, u32[]{:S(2)}, u32[]{:S(2)}) collective-permute-start(bf16[32,512]{1,0:T(8,128)(2,1)S(1)} %collective-permute-done.1), channel_id=1, source_target_pairs={{0,15},{1,0},{2,1},{3,2},{4,3},{5,4},{6,5},{7,6},{8,7},{9,8},{10,9... | collective-permute-start | bytes 98312 | tf_op jit(solution)/shard_map/ppermute | solution.py:77
  253.8 4.1 %collective-permute-start.4 = (bf16[32,512]{1,0:T(8,128)(2,1)S(1)}, bf16[32,512]{1,0:T(8,128)(2,1)S(1)}, u32[]{:S(2)}, u32[]{:S(2)}) collective-permute-start(bf16[32,512]{1,0:T(8,128)(2,1)S(1)} %collective-permute-done.2), channel_id=1, source_target_pairs={{0,1},{1,2},{2,3},{3,4},{4,5},{5,6},{6,7},{7,8},{8,9},{9,10},{10,1... | collective-permute-start | bytes 98312 | tf_op jit(solution)/shard_map/ppermute | solution.py:70
  256.4 3.3 %collective-permute-start.5 = (bf16[32,512]{1,0:T(8,128)(2,1)S(1)}, bf16[32,512]{1,0:T(8,128)(2,1)S(1)}, u32[]{:S(2)}, u32[]{:S(2)}) collective-permute-start(bf16[32,512]{1,0:T(8,128)(2,1)S(1)} %collective-permute-done.3), channel_id=1, source_target_pairs={{0,15},{1,0},{2,1},{3,2},{4,3},{5,4},{6,5},{7,6},{8,7},{9,8},{10,9... | collective-permute-start | bytes 98312 | tf_op jit(solution)/shard_map/ppermute | solution.py:77
  257.9 4.6 %collective-permute-start.6 = (bf16[32,512]{1,0:T(8,128)(2,1)S(1)}, bf16[32,512]{1,0:T(8,128)(2,1)S(1)}, u32[]{:S(2)}, u32[]{:S(2)}) collective-permute-start(bf16[32,512]{1,0:T(8,128)(2,1)S(1)} %collective-permute-done.4), channel_id=1, source_target_pairs={{0,1},{1,2},{2,3},{3,4},{4,5},{5,6},{6,7},{7,8},{8,9},{9,10},{10,1... | collective-permute-start | bytes 98312 | tf_op jit(solution)/shard_map/ppermute | solution.py:70
  259.8 3.3 %collective-permute-start.7 = (bf16[32,512]{1,0:T(8,128)(2,1)S(1)}, bf16[32,512]{1,0:T(8,128)(2,1)S(1)}, u32[]{:S(2)}, u32[]{:S(2)}) collective-permute-start(bf16[32,512]{1,0:T(8,128)(2,1)S(1)} %collective-permute-done.5), channel_id=1, source_target_pairs={{0,15},{1,0},{2,1},{3,2},{4,3},{5,4},{6,5},{7,6},{8,7},{9,8},{10,9... | collective-permute-start | bytes 98312 | tf_op jit(solution)/shard_map/ppermute | solution.py:77
  262.5 4.6 %collective-permute-start.8 = (bf16[32,512]{1,0:T(8,128)(2,1)S(1)}, bf16[32,512]{1,0:T(8,128)(2,1)S(1)}, u32[]{:S(2)}, u32[]{:S(2)}) collective-permute-start(bf16[32,512]{1,0:T(8,128)(2,1)S(1)} %collective-permute-done.6), channel_id=1, source_target_pairs={{0,1},{1,2},{2,3},{3,4},{4,5},{5,6},{6,7},{7,8},{8,9},{9,10},{10,1... | collective-permute-start | bytes 98312 | tf_op jit(solution)/shard_map/ppermute | solution.py:70
  263.1 4.1 %collective-permute-start.9 = (bf16[32,512]{1,0:T(8,128)(2,1)S(1)}, bf16[32,512]{1,0:T(8,128)(2,1)S(1)}, u32[]{:S(2)}, u32[]{:S(2)}) collective-permute-start(bf16[32,512]{1,0:T(8,128)(2,1)S(1)} %collective-permute-done.7), channel_id=1, source_target_pairs={{0,15},{1,0},{2,1},{3,2},{4,3},{5,4},{6,5},{7,6},{8,7},{9,8},{10,9... | collective-permute-start | bytes 98312 | tf_op jit(solution)/shard_map/ppermute | solution.py:77
  267.0 4.6 %collective-permute-start.10 = (bf16[32,512]{1,0:T(8,128)(2,1)S(1)}, bf16[32,512]{1,0:T(8,128)(2,1)S(1)}, u32[]{:S(2)}, u32[]{:S(2)}) collective-permute-start(bf16[32,512]{1,0:T(8,128)(2,1)S(1)} %collective-permute-done.8), channel_id=1, source_target_pairs={{0,1},{1,2},{2,3},{3,4},{4,5},{5,6},{6,7},{7,8},{8,9},{9,10},{10,1... | collective-permute-start | bytes 98312 | tf_op jit(solution)/shard_map/ppermute | solution.py:70
  267.2 4.6 %collective-permute-start.11 = (bf16[32,512]{1,0:T(8,128)(2,1)S(1)}, bf16[32,512]{1,0:T(8,128)(2,1)S(1)}, u32[]{:S(2)}, u32[]{:S(2)}) collective-permute-start(bf16[32,512]{1,0:T(8,128)(2,1)S(1)} %collective-permute-done.9), channel_id=1, source_target_pairs={{0,15},{1,0},{2,1},{3,2},{4,3},{5,4},{6,5},{7,6},{8,7},{9,8},{10,9... | collective-permute-start | bytes 98312 | tf_op jit(solution)/shard_map/ppermute | solution.py:77
  271.6 4.6 %collective-permute-start.12 = (bf16[32,512]{1,0:T(8,128)(2,1)S(1)}, bf16[32,512]{1,0:T(8,128)(2,1)S(1)}, u32[]{:S(2)}, u32[]{:S(2)}) collective-permute-start(bf16[32,512]{1,0:T(8,128)(2,1)S(1)} %collective-permute-done.10), channel_id=1, source_target_pairs={{0,1},{1,2},{2,3},{3,4},{4,5},{5,6},{6,7},{7,8},{8,9},{9,10},{10,1... | collective-permute-start | bytes 98312 | tf_op jit(solution)/shard_map/ppermute | solution.py:70
  271.7 4.6 %collective-permute-start.13 = (bf16[32,512]{1,0:T(8,128)(2,1)S(1)}, bf16[32,512]{1,0:T(8,128)(2,1)S(1)}, u32[]{:S(2)}, u32[]{:S(2)}) collective-permute-start(bf16[32,512]{1,0:T(8,128)(2,1)S(1)} %collective-permute-done.11), channel_id=1, source_target_pairs={{0,15},{1,0},{2,1},{3,2},{4,3},{5,4},{6,5},{7,6},{8,7},{9,8},{10,9... | collective-permute-start | bytes 98312 | tf_op jit(solution)/shard_map/ppermute | solution.py:77
  276.1 4.6 %collective-permute-start.14 = (bf16[32,512]{1,0:T(8,128)(2,1)S(1)}, bf16[32,512]{1,0:T(8,128)(2,1)S(1)}, u32[]{:S(2)}, u32[]{:S(2)}) collective-permute-start(bf16[32,512]{1,0:T(8,128)(2,1)S(1)} %collective-permute-done.12), channel_id=1, source_target_pairs={{0,1},{1,2},{2,3},{3,4},{4,5},{5,6},{6,7},{7,8},{8,9},{9,10},{10,1... | collective-permute-start | bytes 98312 | tf_op jit(solution)/shard_map/ppermute | solution.py:70
  (5 other events, 6.3 us)
Sparse Core Ops, SparseCore 0:
  113.0 80.5 all-gather.2
